TPU v7x, 32 devices: a whole 2x2x4 slice. The times are simulated.
32 devices in a mesh: row: 2 (over y), col: 16 (over z, x, core).
Axes of the slice: x: 2, y: 2, z: 4, core: 2. Of those that a mesh axis runs over, the one named last changes fastest.
Arguments:
- active_matrix: float32 [16384, 16384], P('row', 'col'), may hold values from -6 to 6
- schur_rows: float32 [512, 16384], P('row', 'col'), may hold values from -6 to 6
- accum_first: float32 [32, 512, 512], P('row', 'col'), may hold values from -1 to 1, as said below
- accum_second: float32 [32, 512, 512], P('row', 'col'), may hold values from -1 to 1, as said below
Outputs:
- matrix_out: float32 [16384, 16384], P('row', 'col')
- schur_out: float32 [512, 16384], P('row', 'col')
Inputs may be any that keep to these rules, and one draw needn't show every extreme that they name: `accum_first`: each of the 32 blocks of order 512 is an orthogonal matrix. `accum_second`: each of the 32 blocks of order 512 is an orthogonal matrix.
All inputs are finite; a program needn't handle non-finite values.
Results may differ from a plain program's by a relative error of at most 0.000098.
Values sent between devices are 32-bit elements; how exact they have to be, the bound alone decides.
No kernel may reach another device: no remote copies, remote signals or barrier semaphores. Data moves between devices by JAX's collectives and lax.ppermute only.
A program may use at most 256 MiB of HBM per device.

v0:
```python
import jax
import jax.numpy as jnp
from jax import lax
from jax.sharding import PartitionSpec as P


def spread(array, axis, root):
    mine = lax.axis_index(axis) == root
    return lax.psum(jnp.where(mine, array, jnp.zeros_like(array)), axis)


def passed_along(block, axis, distance):
    devices = range(lax.axis_size(axis))
    route = [((i - distance) % len(devices), i) for i in devices]
    return lax.ppermute(block, axis, route)


def padded(block, sides, width):
    for axis, dim in sides:
        count = lax.axis_size(axis)
        forward = [(i, i + 1) for i in range(count - 1)]
        forward.append((count - 1, 0))
        backward = [(target, source) for source, target in forward]
        low = lax.ppermute(
            lax.slice_in_dim(block, block.shape[dim] - width, None, axis=dim), axis, forward
        )
        high = lax.ppermute(lax.slice_in_dim(block, 0, width, axis=dim), axis, backward)
        block = jnp.concatenate([low, block, high], axis=dim)
    return block


def exact_dot(left, right):
    return jnp.dot(left, right, precision=lax.Precision.HIGHEST, preferred_element_type=jnp.float32)


def aligned_right(matrix, blocks):
    rows, cols = matrix.shape
    count, width = (blocks.shape[0], blocks.shape[1])
    shaped = matrix.reshape(rows, count, width)
    out = jnp.einsum("nki,kij->nkj", shaped, blocks, precision=lax.Precision.HIGHEST)
    return out.reshape(rows, cols)


def straddle_right(extended, blocks, half):
    rows = extended.shape[0]
    width = blocks.shape[1]
    count = blocks.shape[0] - 1
    head = exact_dot(extended[:, :width], blocks[0][:, half:])
    tail = exact_dot(extended[:, count * width :], blocks[count][:, :half])
    pieces = [head]
    if count > 1:
        inner = extended[:, width : count * width].reshape(rows, count - 1, width)
        middle = jnp.einsum("nki,kij->nkj", inner, blocks[1:count], precision=lax.Precision.HIGHEST)
        pieces.append(middle.reshape(rows, (count - 1) * width))
    pieces.append(tail)
    return jnp.concatenate(pieces, axis=1)


def straddle_left(blocks, extended, half):
    cols = extended.shape[1]
    width = blocks.shape[1]
    count = blocks.shape[0] - 1
    head = jnp.einsum(
        "ij,in->jn", blocks[0][:, half:], extended[:width], precision=lax.Precision.HIGHEST
    )
    tail = jnp.einsum(
        "ij,in->jn",
        blocks[count][:, :half],
        extended[count * width :],
        precision=lax.Precision.HIGHEST,
    )
    pieces = [head]
    inner = extended[width : count * width].reshape(count - 1, width, cols)
    middle = jnp.einsum("kij,kin->kjn", blocks[1:count], inner, precision=lax.Precision.HIGHEST)
    pieces.append(middle.reshape((count - 1) * width, cols))
    pieces.append(tail)
    return jnp.concatenate(pieces, axis=0)


def per_device(active_matrix, schur_rows, accum_first, accum_second):
    width = accum_first.shape[2]
    half = width // 2
    row_tile, col_tile = active_matrix.shape
    per_row = row_tile // width
    per_col = col_tile // width
    col_index = lax.axis_index("col")
    owner_row = col_index * per_col // per_row
    owner_offset = col_index * per_col % per_row
    first_full = lax.all_gather(accum_first, "col", axis=1, tiled=True)
    shaped = active_matrix.reshape(per_row, width, col_tile)
    turned_rows = jnp.einsum(
        "kij,kin->kjn", first_full, shaped, precision=lax.Precision.HIGHEST
    ).reshape(row_tile, col_tile)
    chosen = lax.dynamic_slice_in_dim(first_full, owner_offset, per_col, 0)
    first_cols = spread(chosen, "row", owner_row)
    stacked = jnp.concatenate([turned_rows, schur_rows], axis=0)
    turned = aligned_right(stacked, first_cols)
    second_full = lax.all_gather(accum_second, "col", axis=1, tiled=True)
    chosen_second = lax.dynamic_slice_in_dim(second_full, owner_offset, per_col, 0)
    second_cols = spread(chosen_second, "row", owner_row)
    next_col = passed_along(second_cols[0:1], "col", -1)
    col_blocks = jnp.concatenate([second_cols, next_col], axis=0)
    next_row = passed_along(second_full[0:1], "row", -1)
    row_blocks = jnp.concatenate([second_full, next_row], axis=0)
    extended = padded(turned, (("col", 1),), half)
    moved = straddle_right(extended, col_blocks, half)
    matrix_part = moved[:row_tile]
    schur_out = moved[row_tile:]
    extended_rows = padded(matrix_part, (("row", 0),), half)
    matrix_out = straddle_left(row_blocks, extended_rows, half)
    return (matrix_out, schur_out)


def solution(mesh):
    in_specs = (P("row", "col"), P("row", "col"), P("row", "col", None), P("row", "col", None))
    out_specs = (P("row", "col"), P("row", "col"))
    return jax.shard_map(
        per_device, mesh=mesh, in_specs=in_specs, out_specs=out_specs, check_vma=False
    )
```

profile of v0, /device:TPU:1, one launch (start us, length us, event | category | flops | bytes accessed | tf_op | source)
XLA Modules:
  0.0 975.9 jit_solution(12555701314665027359)
XLA Ops:
  7.2 0.0 all-gather.3.cloned.1.call-start
  7.2 0.7 all-gather.3.cloned.1.call-update
  7.9 0.0 all-gather.5.cloned.1.call-start
  7.9 0.7 all-gather.5.cloned.1.call-update
  8.6 0.0 all-reduce.3.cloned.1.call-start
  8.7 130.4 %all-gather.3.cloned.1.call-done = f32[16,512,512]{2,1,0:T(8,128)} async-done(((f32[16,32,512]{2,1,0:T(8,128)}), f32[16,512,512]{2,1,0:T(8,128)}) %all-gather.3.cloned.1.call-update) | async-done | bytes 16777232 | tf_op jit(solution)/shard_map/all_gather | solution.py:89
  139.1 3.2 dynamic-slice_select_fusion.1
  142.3 123.7 %all-gather.5.cloned.1.call-done = f32[16,512,512]{2,1,0:T(8,128)} async-done(((f32[16,32,512]{2,1,0:T(8,128)}), f32[16,512,512]{2,1,0:T(8,128)}) %all-gather.5.cloned.1.call-update) | async-done | bytes 16777232 | tf_op jit(solution)/shard_map/all_gather | solution.py:98
  266.0 3.1 dynamic-slice_select_fusion
  269.1 0.0 all-reduce.3.cloned.1.call-update
  269.1 1.6 copy.11
  270.7 0.3 copy.13
  271.0 60.6 %fusion.31 = f32[16,512,1024]{2,1,0:T(8,128)} fusion(f32[16,512,512]{2,1,0:T(8,128)} %all-gather.3.cloned.1.call-done, f32[16,512,1024]{2,1,0:T(8,128)} %bitcast.40), kind=kOutput, calls=%fused_computation.43 | convolution fusion | flops 51539607552 | bytes 83886080 | tf_op jit(solution)/shard_map/kij,kin->kjn/dot_general | solution.py:91
  331.6 42.7 %concatenate.28 = f32[8192,2,512]{2,1,0:T(2,128)} reshape(f32[16,512,1024]{2,1,0:T(8,128)} %fusion.31) | data formatting | bytes 67108864 | tf_op jit(solution)/shard_map/concatenate | solution.py:96
  374.3 27.6 %copy.12 = f32[8192,2,512]{2,0,1:T(8,128)} copy(f32[8192,2,512]{2,1,0:T(2,128)} %concatenate.28) | data formatting | bytes 67108864 | tf_op jit(solution)/shard_map/concatenate | solution.py:96
  401.9 0.0 all-reduce.3.cloned.1.call-done
  401.9 115.2 %fusion = f32[2,512,8448]{2,1,0:T(8,128)} fusion(f32[2,512,512]{2,1,0:T(8,128)} %get-tuple-element.6, f32[256,2,512]{2,0,1:T(8,128)S(1)} %copy.13, f32[8192,2,512]{2,0,1:T(8,128)} %copy.12), kind=kOutput, calls=%fused_computation | convolution fusion | flops 53158871040 | bytes 71303168 | tf_op jit(solution)/shard_map/nki,kij->nkj/dot_general | solution.py:40
  517.1 0.0 copy-start.2
  517.1 12.2 %fusion.30 = (f32[8448,256]{0,1:T(8,128)}, f32[8448,256]{0,1:T(8,128)}) fusion(f32[8448,1024]{0,1:T(8,128)} %bitcast.34), kind=kLoop, calls=%fused_computation.42 | loop fusion | bytes 34603008 | tf_op jit(solution)/shard_map/slice | solution.py:25
  529.3 0.4 collective-permute-start.1
  529.7 1.3 collective-permute-start
  531.0 2.9 slice_bitcast_fusion.2
  533.9 1.2 collective-permute-start.5
  535.1 0.0 copy-done.2
  535.2 0.1 slice_bitcast_fusion.3
  535.3 0.1 collective-permute-start.2
  535.4 34.6 %fusion.12 = f32[8448,512]{0,1:T(8,128)S(1)} fusion(f32[8448,1024]{0,1:T(8,128)} %bitcast.35, f32[2,512,512]{2,1,0:T(8,128)S(1)} %copy-done.2), kind=kOutput, calls=%fused_computation.16 | convolution fusion | flops 26575110144 | bytes 35651584 | tf_op jit(solution)/shard_map/nki,kij->nkj/dot_general | solution.py:53
  570.0 0.0 copy-start.1
  570.0 159.1 %collective-permute-done.2 = f32[1,512,512]{2,1,0:T(8,128)S(1)} collective-permute-done((f32[1,512,512]{2,1,0:T(8,128)S(1)}, f32[1,512,512]{2,1,0:T(8,128)S(1)}, u32[]{:S(2)}, u32[]{:S(2)}) %collective-permute-start.2) | collective-permute-done | bytes 1048608 | tf_op jit(solution)/shard_map/ppermute | solution.py:15
  729.1 0.0 copy-start.4
  729.1 1.0 copy-done.4
  730.1 0.0 collective-permute-done.1
  730.1 20.4 %fusion.4 = f32[8448,256]{0,1:T(8,128)} fusion(f32[8448,256]{0,1:T(8,128)} %collective-permute-done.1, f32[8448,1024]{0,1:T(8,128)} %bitcast.36, f32[512,512]{1,0:T(8,128)} %bitcast.42), kind=kOutput, calls=%fused_computation.7 | convolution fusion | flops 13291880448 | bytes 52428800 | tf_op jit(solution)/shard_map/dot_general | solution.py:33
  750.5 0.0 collective-permute-done
  750.5 20.5 %fusion.8 = f32[8448,256]{0,1:T(8,128)} fusion(f32[8448,1024]{0,1:T(8,128)} %bitcast.37, f32[8448,256]{0,1:T(8,128)} %collective-permute-done, f32[512,512]{1,0:T(8,128)S(1)} %get-tuple-element.15), kind=kOutput, calls=%fused_computation.12 | convolution fusion | flops 13291880448 | bytes 52428800 | tf_op jit(solution)/shard_map/dot_general | solution.py:33
  771.1 0.0 copy-done.1
  771.1 1.6 pad_maximum_fusion.14
  772.7 23.2 %pad_maximum_fusion = f32[8448,1024]{0,1:T(8,128)} fusion(f32[8448,256]{0,1:T(8,128)} %fusion.4, f32[8448,512]{0,1:T(8,128)} %copy-done.1, f32[8448,256]{0,1:T(8,128)} %fusion.8), kind=kLoop, calls=%fused_computation.4 | loop fusion | flops 17301504 | bytes 69206016 | tf_op jit(solution)/shard_map/concatenate | solution.py:56
  795.9 1.2 collective-permute-start.4
  797.1 21.7 %slice.99 = f32[7680,1024]{0,1:T(8,128)} slice(f32[8448,1024]{0,1:T(8,128)} %pad_maximum_fusion), slice={[256:7936], [0:1024]} | slice | bytes 62914560 | tf_op jit(solution)/shard_map/slice | solution.py:73
  818.8 31.3 %copy.15 = f32[7680,1024]{1,0:T(8,128)} copy(f32[7680,1024]{0,1:T(8,128)} %slice.99) | data formatting | bytes 62914560 | tf_op jit(solution)/shard_map/slice | solution.py:73
  850.1 0.2 collective-permute-start.3
  850.3 57.9 %fusion.10 = f32[15,1024,512]{1,2,0:T(8,128)} fusion(f32[15,512,1024]{2,1,0:T(8,128)} %bitcast.39, f32[16,512,512]{2,1,0:T(8,128)} %all-gather.5.cloned.1.call-done), kind=kOutput, calls=%fused_computation.14 | convolution fusion | flops 48318382080 | bytes 78643200 | tf_op jit(solution)/shard_map/kij,kin->kjn/dot_general | solution.py:74
  908.2 23.0 %slice.96 = f32[8192,1024]{0,1:T(8,128)} slice(f32[8448,1024]{0,1:T(8,128)} %pad_maximum_fusion), slice={[0:8192], [0:1024]} | slice | bytes 67108864 | tf_op jit(solution)/shard_map/slice | solution.py:107
  931.2 1.3 copy.17
  932.5 0.0 collective-permute-done.5
  932.5 0.0 collective-permute-done.4
  932.5 0.0 copy-start
  932.5 0.0 copy-start.3
  932.5 3.8 fusion.20
  936.3 0.0 collective-permute-done.3
  936.3 7.5 copy-done
  943.9 0.2 copy-done.3
  944.1 3.3 fusion.19
  947.4 21.8 %pad_maximum_fusion.1 = f32[8192,1024]{1,0:T(8,128)} fusion(f32[256,1024]{1,0:T(8,128)S(1)} %fusion.20, f32[7680,1024]{1,0:T(8,128)} %bitcast.38, f32[256,1024]{1,0:T(8,128)S(1)} %fusion.19), kind=kLoop, calls=%fused_computation.5 | loop fusion | flops 16777216 | bytes 67108864 | tf_op jit(solution)/shard_map/concatenate | solution.py:77
Async XLA Ops:
  7.2 132.0 %all-gather.3.cloned.1.call-start = ((), (), s32[]{:S(2)}) async-start(), calls=%async_computation | async-start | bytes 17825792 | tf_op jit(solution)/shard_map/all_gather | solution.py:89
  7.9 258.1 %all-gather.5.cloned.1.call-start = ((), (), s32[]{:S(2)}) async-start(), calls=%async_computation.1 | async-start | bytes 17825792 | tf_op jit(solution)/shard_map/all_gather | solution.py:98
  8.6 393.3 %all-reduce.3.cloned.1.call-start = ((), (), s32[]{:S(2)}) async-start(), calls=%async_computation.2 | async-start | bytes 8388608 | tf_op jit(solution)/shard_map/psum | solution.py:9
  517.1 18.1 %copy-start.2 = (f32[2,512,512]{2,1,0:T(8,128)S(1)}, f32[2,512,512]{2,1,0:T(8,128)}, u32[]{:S(2)}) copy-start(f32[2,512,512]{2,1,0:T(8,128)} %get-tuple-element.7) | copy-start | bytes 6291460
  529.3 200.8 %collective-permute-start.1 = (f32[8448,256]{0,1:T(8,128)}, f32[8448,256]{0,1:T(8,128)}, u32[]{:S(2)}, u32[]{:S(2)}) collective-permute-start(f32[8448,256]{0,1:T(8,128)} %get-tuple-element.12), channel_id=1, source_target_pairs={{1,0},{2,1},{3,2},{4,3},{5,4},{6,5},{7,6},{8,7},{9,8},{10,9},{11,1... | collective-permute-start | bytes 25952264 | tf_op jit(solution)/shard_map/ppermute | solution.py:27
  529.7 220.8 %collective-permute-start = (f32[8448,256]{0,1:T(8,128)}, f32[8448,256]{0,1:T(8,128)}, u32[]{:S(2)}, u32[]{:S(2)}) collective-permute-start(f32[8448,256]{0,1:T(8,128)} %get-tuple-element.11), channel_id=1, source_target_pairs={{0,1},{1,2},{2,3},{3,4},{4,5},{5,6},{6,7},{7,8},{8,9},{9,10},{10,1... | collective-permute-start | bytes 25952264 | tf_op jit(solution)/shard_map/ppermute | solution.py:24
  533.9 398.6 %collective-permute-start.5 = (f32[1,512,512]{2,1,0:T(8,128)}, f32[1,512,512]{2,1,0:T(8,128)}, u32[]{:S(2)}, u32[]{:S(2)}) collective-permute-start(f32[1,512,512]{2,1,0:T(8,128)} %get-tuple-element.14), channel_id=1, source_target_pairs={{16,0},{0,16},{17,1},{1,17},{18,2},{2,18},{19,3},{3,19},{20,4},{4,... | collective-permute-start | bytes 3145736 | tf_op jit(solution)/shard_map/ppermute | solution.py:15
  535.3 193.8 %collective-permute-start.2 = (f32[1,512,512]{2,1,0:T(8,128)S(1)}, f32[1,512,512]{2,1,0:T(8,128)S(1)}, u32[]{:S(2)}, u32[]{:S(2)}) collective-permute-start(f32[1,512,512]{2,1,0:T(8,128)S(1)} %get-tuple-element.16), channel_id=1, source_target_pairs={{1,0},{2,1},{3,2},{4,3},{5,4},{6,5},{7,6},{8,7},{9,8},{10,9},{11,1... | collective-permute-start | bytes 3145736 | tf_op jit(solution)/shard_map/ppermute | solution.py:15
  570.0 201.1 %copy-start.1 = (f32[8448,512]{0,1:T(8,128)}, f32[8448,512]{0,1:T(8,128)S(1)}, u32[]{:S(2)}) copy-start(f32[8448,512]{0,1:T(8,128)S(1)} %fusion.12) | copy-start | bytes 51904516
  729.1 1.0 copy-start.4
  795.9 136.6 %collective-permute-start.4 = (f32[256,1024]{0,1:T(8,128)S(1)}, f32[256,1024]{0,1:T(8,128)}, u32[]{:S(2)}, u32[]{:S(2)}) collective-permute-start(f32[256,1024]{0,1:T(8,128)S(1)} %get-tuple-element.9), channel_id=1, source_target_pairs={{16,0},{0,16},{17,1},{1,17},{18,2},{2,18},{19,3},{3,19},{20,4},{4,... | collective-permute-start | bytes 3145736 | tf_op jit(solution)/shard_map/ppermute | solution.py:27
  850.1 86.3 %collective-permute-start.3 = (f32[256,1024]{0,1:T(8,128)S(1)}, f32[256,1024]{0,1:T(8,128)}, u32[]{:S(2)}, u32[]{:S(2)}) collective-permute-start(f32[256,1024]{0,1:T(8,128)S(1)} %get-tuple-element.10), channel_id=1, source_target_pairs={{0,16},{16,0},{1,17},{17,1},{2,18},{18,2},{3,19},{19,3},{4,20},{20... | collective-permute-start | bytes 3145736 | tf_op jit(solution)/shard_map/ppermute | solution.py:24
  932.5 11.3 %copy-start = (f32[8192,1024]{0,1:T(8,128)S(1)}, f32[8192,1024]{0,1:T(8,128)}, u32[]{:S(2)}) copy-start(f32[8192,1024]{0,1:T(8,128)} %slice.96) | copy-start | bytes 100663296
  932.5 11.6 %copy-start.3 = (f32[512,512]{1,0:T(8,128)S(1)}, f32[512,512]{1,0:T(8,128)}, u32[]{:S(2)}) copy-start(f32[512,512]{1,0:T(8,128)} %get-tuple-element.13) | copy-start | bytes 3145732
Sparse Core Ops, SparseCore 0:
  10.2 128.9 all-gather.2
  141.3 124.6 all-gather.4
  269.2 105.5 all-reduce.2
where the time goes:
time: 986 us; the launch traced here: 976 us
  waiting for transfers between devices  415 us (42%)
  matrix products  316 us (32%)
  local copies, waits for them, and re-layouts  173 us (18%)
  other arithmetic  52.9 us (5%)
  between operations  14.1 us (1%)
    ppermute x2, waiting for transfers between devices, passed_along(): return lax.ppermute(block, axis, route)  159 us
    all_gather x1, waiting for transfers between devices, per_device(): first_full = lax.all_gather(accum_first, 'col', axis=1, tiled=True)  130 us
    all_gather x1, waiting for transfers between devices, per_device(): second_full = lax.all_gather(accum_second, 'col', axis=1, tiled=True)  124 us
    dot_general x1, matrix products, aligned_right(): jnp.einsum('nki,kij->nkj', shaped, blocks, precision=lax.Precision.HIGHEST)  115 us
    concatenate x3, local copies, waits for them, and re-layouts, per_device(): stacked = jnp.concatenate([turned_rows, schur_rows], axis=0)  70.6 us
    dot_general x1, matrix products, per_device(): jnp.einsum('kij,kin->kjn', first_full, shaped, precision=lax.Precision.HI...  60.6 us
    dot_general x1, matrix products, straddle_left(): jnp.einsum('kij,kin->kjn', blocks[1:count], inner, precision=lax.Precisio...  57.9 us
    slice x2, local copies, waits for them, and re-layouts, straddle_left(): inner = extended[width:count * width].reshape(count - 1, width, cols)  53 us
  transfers between devices with their start and end apart: 9, of which 3 were waited for; matrix products, arithmetic and copies ran while one was open for 39% of the time, Pallas kernels for 0%

commit v1 on v0

--- a/solution.py
+++ b/solution.py
@@ -2,6 +2,16 @@
 import jax.numpy as jnp
 from jax import lax
 from jax.sharding import PartitionSpec as P
+
+
+def pass_along(array, name, along):
+    devices = lax.axis_size(name)
+    held, tiles = (array, [array])
+    for _ in range(devices - 1):
+        held = lax.ppermute(held, name, [(i, (i + 1) % devices) for i in range(devices)])
+        tiles.insert(0, held)
+    line = jnp.concatenate(tiles, axis=along)
+    return jnp.roll(line, (lax.axis_index(name) + 1) * array.shape[along], axis=along)
 
 
 def spread(array, axis, root):
@@ -95,7 +105,7 @@
     first_cols = spread(chosen, "row", owner_row)
     stacked = jnp.concatenate([turned_rows, schur_rows], axis=0)
     turned = aligned_right(stacked, first_cols)
-    second_full = lax.all_gather(accum_second, "col", axis=1, tiled=True)
+    second_full = pass_along(accum_second, "col", 1)
     chosen_second = lax.dynamic_slice_in_dim(second_full, owner_offset, per_col, 0)
     second_cols = spread(chosen_second, "row", owner_row)
     next_col = passed_along(second_cols[0:1], "col", -1)

time: 986 us -> 1250 us (1.27)
  matrix products: 316 us -> 482 us
  local copies, waits for them, and re-layouts: 173 us -> 229 us
  starting transfers between devices: 4.62 us -> 31.9 us
  waiting for transfers between devices: 415 us -> 428 us
    ppermute x0 -> x15, waiting for transfers between devices: none -> 307 us  [pass_along(): lax.ppermute(held, name, [(i, (i + 1) % devices) for i in range(devices)])]
    dot_general x1, matrix products: 57.9 us -> 221 us  [straddle_left(): jnp.einsum('kij,kin->kjn', blocks[1:count], inner, precision=lax.Precisio...]
    ppermute x2, waiting for transfers between devices: 159 us -> 0.01 us  [passed_along(): return lax.ppermute(block, axis, route)]
    all_gather x1, waiting for transfers between devices: 130 us -> 0.01 us  [per_device(): first_full = lax.all_gather(accum_first, 'col', axis=1, tiled=True)]
    all_gather x1 -> x0, waiting for transfers between devices: 124 us -> none  [per_device(): second_full = lax.all_gather(accum_second, 'col', axis=1, tiled=True)]
    ppermute x2, waiting for transfers between devices: 0.01 us -> 121 us  [padded(): lax.ppermute(lax.slice_in_dim(block, block.shape[dim] - width, None, axis...]
    unnamed x12 -> x91, local copies, waits for them, and re-layouts: 11.6 us -> 53.3 us
    ppermute x2, starting transfers between devices: 1.66 us -> 16.2 us  [padded(): lax.ppermute(lax.slice_in_dim(block, 0, width, axis=dim), axis, backward)]
  transfers between devices with their start and end apart: 9 -> 23, of which waited for: 3 -> 16; matrix products, arithmetic and copies ran while one was open for 39% -> 47% of each run, Pallas kernels for 0% -> 0%
where the time goes in v1:
time: 1250 us; the launch traced here: 1240 us
  matrix products  482 us (39%)
  waiting for transfers between devices  428 us (34%)
  local copies, waits for them, and re-layouts  229 us (18%)
  other arithmetic  52.8 us (4%)
  starting transfers between devices  31.9 us (3%)
  between operations  15 us (1%)
    ppermute x15, waiting for transfers between devices, pass_along(): lax.ppermute(held, name, [(i, (i + 1) % devices) for i in range(devices)])  307 us
    dot_general x1, matrix products, straddle_left(): jnp.einsum('kij,kin->kjn', blocks[1:count], inner, precision=lax.Precisio...  221 us
    ppermute x2, waiting for transfers between devices, padded(): lax.ppermute(lax.slice_in_dim(block, block.shape[dim] - width, None, axis...  121 us
    dot_general x1, matrix products, aligned_right(): jnp.einsum('nki,kij->nkj', shaped, blocks, precision=lax.Precision.HIGHEST)  115 us
    concatenate x3, local copies, waits for them, and re-layouts, per_device(): stacked = jnp.concatenate([turned_rows, schur_rows], axis=0)  70.9 us
    dot_general x1, matrix products, per_device(): jnp.einsum('kij,kin->kjn', first_full, shaped, precision=lax.Precision.HI...  60.1 us
    unnamed x91, local copies, waits for them, and re-layouts  53.3 us
    slice x2, local copies, waits for them, and re-layouts, straddle_left(): inner = extended[width:count * width].reshape(count - 1, width, cols)  52.6 us
  transfers between devices with their start and end apart: 23, of which 16 were waited for; matrix products, arithmetic and copies ran while one was open for 47% of the time, Pallas kernels for 0%

profile of v1, /device:TPU:1, one launch (start us, length us, event | category | flops | bytes accessed | tf_op | source)
XLA Modules:
  0.0 1239.2 jit_solution(16145435463312079897)
XLA Ops:
  8.0 2.6 collective-permute-start
  10.6 14.2 %collective-permute-done = f32[16,32,512]{2,1,0:T(8,128)S(1)} collective-permute-done((f32[16,32,512]{2,1,0:T(8,128)}, f32[16,32,512]{2,1,0:T(8,128)S(1)}, u32[]{:S(2)}, u32[]{:S(2)}) %collective-permute-start) | collective-permute-done | bytes 1048608 | tf_op jit(solution)/shard_map/ppermute | solution.py:11
  24.8 2.4 collective-permute-start.1
  27.2 17.8 %collective-permute-done.1 = f32[16,32,512]{2,1,0:T(8,128)S(1)} collective-permute-done((f32[16,32,512]{2,1,0:T(8,128)S(1)}, f32[16,32,512]{2,1,0:T(8,128)S(1)}, u32[]{:S(2)}, u32[]{:S(2)}) %collective-permute-start.1) | collective-permute-done | bytes 1048608 | tf_op jit(solution)/shard_map/ppermute | solution.py:11
  45.0 2.5 collective-permute-start.2
  47.5 20.4 %collective-permute-done.2 = f32[16,32,512]{2,1,0:T(8,128)S(1)} collective-permute-done((f32[16,32,512]{2,1,0:T(8,128)S(1)}, f32[16,32,512]{2,1,0:T(8,128)S(1)}, u32[]{:S(2)}, u32[]{:S(2)}) %collective-permute-start.2) | collective-permute-done | bytes 1048608 | tf_op jit(solution)/shard_map/ppermute | solution.py:11
  69.0 24.1 %collective-permute-done.3 = f32[16,32,512]{2,1,0:T(8,128)S(1)} collective-permute-done((f32[16,32,512]{2,1,0:T(8,128)S(1)}, f32[16,32,512]{2,1,0:T(8,128)S(1)}, u32[]{:S(2)}, u32[]{:S(2)}) %collective-permute-start.3) | collective-permute-done | bytes 1048608 | tf_op jit(solution)/shard_map/ppermute | solution.py:11
  94.1 1.6 collective-permute-start.4
  95.6 37.9 %collective-permute-done.4 = f32[16,32,512]{2,1,0:T(8,128)S(1)} collective-permute-done((f32[16,32,512]{2,1,0:T(8,128)S(1)}, f32[16,32,512]{2,1,0:T(8,128)S(1)}, u32[]{:S(2)}, u32[]{:S(2)}) %collective-permute-start.4) | collective-permute-done | bytes 1048608 | tf_op jit(solution)/shard_map/ppermute | solution.py:11
  134.6 39.5 %collective-permute-done.5 = f32[16,32,512]{2,1,0:T(8,128)S(1)} collective-permute-done((f32[16,32,512]{2,1,0:T(8,128)S(1)}, f32[16,32,512]{2,1,0:T(8,128)S(1)}, u32[]{:S(2)}, u32[]{:S(2)}) %collective-permute-start.5) | collective-permute-done | bytes 1048608 | tf_op jit(solution)/shard_map/ppermute | solution.py:11
  175.1 16.9 %collective-permute-done.6 = f32[16,32,512]{2,1,0:T(8,128)S(1)} collective-permute-done((f32[16,32,512]{2,1,0:T(8,128)S(1)}, f32[16,32,512]{2,1,0:T(8,128)S(1)}, u32[]{:S(2)}, u32[]{:S(2)}) %collective-permute-start.6) | collective-permute-done | bytes 1048608 | tf_op jit(solution)/shard_map/ppermute | solution.py:11
  193.0 16.9 %collective-permute-done.7 = f32[16,32,512]{2,1,0:T(8,128)S(1)} collective-permute-done((f32[16,32,512]{2,1,0:T(8,128)S(1)}, f32[16,32,512]{2,1,0:T(8,128)S(1)}, u32[]{:S(2)}, u32[]{:S(2)}) %collective-permute-start.7) | collective-permute-done | bytes 1048608 | tf_op jit(solution)/shard_map/ppermute | solution.py:11
  210.9 16.9 %collective-permute-done.8 = f32[16,32,512]{2,1,0:T(8,128)S(1)} collective-permute-done((f32[16,32,512]{2,1,0:T(8,128)S(1)}, f32[16,32,512]{2,1,0:T(8,128)S(1)}, u32[]{:S(2)}, u32[]{:S(2)}) %collective-permute-start.8) | collective-permute-done | bytes 1048608 | tf_op jit(solution)/shard_map/ppermute | solution.py:11
  228.8 16.9 %collective-permute-done.9 = f32[16,32,512]{2,1,0:T(8,128)S(1)} collective-permute-done((f32[16,32,512]{2,1,0:T(8,128)S(1)}, f32[16,32,512]{2,1,0:T(8,128)S(1)}, u32[]{:S(2)}, u32[]{:S(2)}) %collective-permute-start.9) | collective-permute-done | bytes 1048608 | tf_op jit(solution)/shard_map/ppermute | solution.py:11
  246.8 16.9 %collective-permute-done.10 = f32[16,32,512]{2,1,0:T(8,128)S(1)} collective-permute-done((f32[16,32,512]{2,1,0:T(8,128)S(1)}, f32[16,32,512]{2,1,0:T(8,128)S(1)}, u32[]{:S(2)}, u32[]{:S(2)}) %collective-permute-start.10) | collective-permute-done | bytes 1048608 | tf_op jit(solution)/shard_map/ppermute | solution.py:11
  264.7 16.9 %collective-permute-done.11 = f32[16,32,512]{2,1,0:T(8,128)S(1)} collective-permute-done((f32[16,32,512]{2,1,0:T(8,128)S(1)}, f32[16,32,512]{2,1,0:T(8,128)S(1)}, u32[]{:S(2)}, u32[]{:S(2)}) %collective-permute-start.11) | collective-permute-done | bytes 1048608 | tf_op jit(solution)/shard_map/ppermute | solution.py:11
  282.5 16.9 %collective-permute-done.12 = f32[16,32,512]{2,1,0:T(8,128)S(1)} collective-permute-done((f32[16,32,512]{2,1,0:T(8,128)S(1)}, f32[16,32,512]{2,1,0:T(8,128)S(1)}, u32[]{:S(2)}, u32[]{:S(2)}) %collective-permute-start.12) | collective-permute-done | bytes 1048608 | tf_op jit(solution)/shard_map/ppermute | solution.py:11
  300.4 17.0 %collective-permute-done.13 = f32[16,32,512]{2,1,0:T(8,128)} collective-permute-done((f32[16,32,512]{2,1,0:T(8,128)S(1)}, f32[16,32,512]{2,1,0:T(8,128)}, u32[]{:S(2)}, u32[]{:S(2)}) %collective-permute-start.13) | collective-permute-done | bytes 1048608 | tf_op jit(solution)/shard_map/ppermute | solution.py:11
  317.6 17.1 %collective-permute-done.14 = f32[16,32,512]{2,1,0:T(8,128)} collective-permute-done((f32[16,32,512]{2,1,0:T(8,128)}, f32[16,32,512]{2,1,0:T(8,128)}, u32[]{:S(2)}, u32[]{:S(2)}) %collective-permute-start.14) | collective-permute-done | bytes 1048608 | tf_op jit(solution)/shard_map/ppermute | solution.py:11
  334.7 1.3 constant_dynamic-update-slice_fusion.31
  336.0 1.3 constant_dynamic-update-slice_fusion.30
  337.4 1.3 constant_dynamic-update-slice_fusion.29
  338.7 1.3 constant_dynamic-update-slice_fusion.28
  340.0 1.3 constant_dynamic-update-slice_fusion.27
  341.4 1.3 constant_dynamic-update-slice_fusion.26
  342.7 1.3 constant_dynamic-update-slice_fusion.25
  344.0 1.3 constant_dynamic-update-slice_fusion.24
  345.4 1.3 constant_dynamic-update-slice_fusion.23
  346.7 1.3 constant_dynamic-update-slice_fusion.22
  348.0 1.3 constant_dynamic-update-slice_fusion.21
  349.3 1.3 constant_dynamic-update-slice_fusion.20
  350.7 1.3 constant_dynamic-update-slice_fusion.19
  352.2 1.3 constant_dynamic-update-slice_fusion.16
  353.5 1.3 constant_dynamic-update-slice_fusion.15
  354.8 1.3 constant_dynamic-update-slice_fusion.14
  357.7 11.1 copy-done.2
  368.7 1.6 dynamic-slice_select_fusion
  370.3 3.2 dynamic-slice_select_fusion.1
  373.5 1.6 copy.11
  375.4 60.1 %fusion.30 = f32[16,512,1024]{2,1,0:T(8,128)} fusion(f32[16,512,512]{2,1,0:T(8,128)} %all-gather.2.cloned.1.call-done, f32[16,512,1024]{2,1,0:T(8,128)} %bitcast.33), kind=kOutput, calls=%fused_computation.74 | convolution fusion | flops 51539607552 | bytes 83886080 | tf_op jit(solution)/shard_map/kij,kin->kjn/dot_general | solution.py:101
  435.5 43.0 %concatenate.35 = f32[8192,2,512]{2,1,0:T(2,128)} reshape(f32[16,512,1024]{2,1,0:T(8,128)} %fusion.30) | data formatting | bytes 67108864 | tf_op jit(solution)/shard_map/concatenate | solution.py:106
  478.5 27.6 %copy.12 = f32[8192,2,512]{2,0,1:T(8,128)} copy(f32[8192,2,512]{2,1,0:T(2,128)} %concatenate.35) | data formatting | bytes 67108864 | tf_op jit(solution)/shard_map/concatenate | solution.py:106
  506.1 115.2 %fusion = f32[2,512,8448]{2,1,0:T(8,128)} fusion(f32[2,512,512]{2,1,0:T(8,128)} %get-tuple-element.6, f32[256,2,512]{2,0,1:T(8,128)S(1)} %copy.13, f32[8192,2,512]{2,0,1:T(8,128)} %copy.12), kind=kOutput, calls=%fused_computation | convolution fusion | flops 53158871040 | bytes 71303168 | tf_op jit(solution)/shard_map/nki,kij->nkj/dot_general | solution.py:50
  621.3 12.2 fusion.29
  633.5 14.9 %collective-permute-start.16 = (f32[8448,256]{0,1:T(8,128)}, f32[8448,256]{0,1:T(8,128)}, u32[]{:S(2)}, u32[]{:S(2)}) collective-permute-start(f32[8448,256]{0,1:T(8,128)} %get-tuple-element.12), channel_id=1, source_target_pairs={{1,0},{2,1},{3,2},{4,3},{5,4},{6,5},{7,6},{8,7},{9,8},{10,9},{11,1... | collective-permute-start | bytes 25952264 | tf_op jit(solution)/shard_map/ppermute | solution.py:37
  648.4 2.3 constant_dynamic-slice_fusion
  650.7 1.6 collective-permute-start.19
  652.3 2.3 fusion.35
  654.6 11.7 fusion.42
  666.5 4.8 collective-permute-start.17
  671.3 34.6 %fusion.12 = f32[8448,512]{0,1:T(8,128)S(1)} fusion(f32[8448,1024]{0,1:T(8,128)} %bitcast.30, f32[2,512,512]{2,1,0:T(8,128)S(1)} %copy-done.3), kind=kOutput, calls=%fused_computation.16 | convolution fusion | flops 26575110144 | bytes 35651584 | tf_op jit(solution)/shard_map/nki,kij->nkj/dot_general | solution.py:63
  705.9 120.8 %collective-permute-done.15 = f32[8448,256]{0,1:T(8,128)} collective-permute-done((f32[8448,256]{0,1:T(8,128)}, f32[8448,256]{0,1:T(8,128)}, u32[]{:S(2)}, u32[]{:S(2)}) %collective-permute-start.15) | collective-permute-done | bytes 8650784 | tf_op jit(solution)/shard_map/ppermute | solution.py:34
  826.7 20.4 %fusion.8 = f32[8448,256]{0,1:T(8,128)} fusion(f32[8448,1024]{0,1:T(8,128)} %bitcast.31, f32[8448,256]{0,1:T(8,128)} %collective-permute-done.15, f32[512,512]{1,0:T(8,128)S(1)} %get-tuple-element.13), kind=kOutput, calls=%fused_computation.12 | convolution fusion | flops 13291880448 | bytes 52428800 | tf_op jit(solution)/shard_map/dot_general | solution.py:43
  847.2 20.5 %fusion.4 = f32[8448,256]{0,1:T(8,128)} fusion(f32[8448,256]{0,1:T(8,128)} %collective-permute-done.16, f32[8448,1024]{0,1:T(8,128)} %bitcast.32, f32[512,512]{1,0:T(8,128)S(1)} %bitcast.37), kind=kOutput, calls=%fused_computation.7 | convolution fusion | flops 13291880448 | bytes 52428800 | tf_op jit(solution)/shard_map/dot_general | solution.py:43
  867.6 3.1 pad_maximum_fusion.10
  870.7 23.1 %pad_maximum_fusion = f32[8448,1024]{0,1:T(8,128)} fusion(f32[8448,256]{0,1:T(8,128)} %fusion.4, f32[8448,512]{0,1:T(8,128)} %copy-done.1, f32[8448,256]{0,1:T(8,128)} %fusion.8), kind=kLoop, calls=%fused_computation.4 | loop fusion | flops 17301504 | bytes 69206016 | tf_op jit(solution)/shard_map/concatenate | solution.py:66
  895.3 21.7 %slice.98 = f32[7680,1024]{0,1:T(8,128)} slice(f32[8448,1024]{0,1:T(8,128)} %pad_maximum_fusion), slice={[256:7936], [0:1024]} | slice | bytes 62914560 | tf_op jit(solution)/shard_map/slice | solution.py:83
  917.0 30.9 %copy.15 = f32[7680,1024]{1,0:T(8,128)} copy(f32[7680,1024]{0,1:T(8,128)} %slice.98) | data formatting | bytes 62914560 | tf_op jit(solution)/shard_map/slice | solution.py:83
  947.9 221.4 %fusion.10 = f32[15,512,1024]{2,1,0:T(8,128)} fusion(f32[15,512,1024]{2,1,0:T(8,128)} %bitcast.35, f32[16,512,512]{2,1,0:T(8,128)} %fusion.42), kind=kOutput, calls=%fused_computation.14 | convolution fusion | flops 48318382080 | bytes 79691776 | tf_op jit(solution)/shard_map/kij,kin->kjn/dot_general | solution.py:84
  1169.3 23.4 %slice.97 = f32[8192,1024]{0,1:T(8,128)} slice(f32[8448,1024]{0,1:T(8,128)} %pad_maximum_fusion), slice={[0:8192], [0:1024]} | slice | bytes 67108864 | tf_op jit(solution)/shard_map/slice | solution.py:117
  1194.0 5.2 fusion.17
  1199.2 6.0 copy-done
  1205.2 4.9 fusion.15
  1210.1 21.8 %pad_maximum_fusion.1 = f32[8192,1024]{1,0:T(8,128)} fusion(f32[256,1024]{1,0:T(8,128)S(1)} %fusion.15, f32[7680,1024]{1,0:T(8,128)} %bitcast.34, f32[256,1024]{1,0:T(8,128)S(1)} %fusion.17), kind=kLoop, calls=%fused_computation.5 | loop fusion | flops 16777216 | bytes 67108864 | tf_op jit(solution)/shard_map/concatenate | solution.py:87
  (100 shorter events, 16.5 us)
Async XLA Ops:
  7.2 350.4 %copy-start.5 = (f32[16,32,512]{2,1,0:T(8,128)S(1)}, f32[16,32,512]{2,1,0:T(8,128)}, u32[]{:S(2)}) copy-start(f32[16,32,512]{2,1,0:T(8,128)} %param.7) | copy-start | bytes 3145732
  7.2 363.1 %all-gather.2.cloned.1.call-start = ((), (), s32[]{:S(2)}) async-start(), calls=%async_computation | async-start | bytes 17825792 | tf_op jit(solution)/shard_map/all_gather | solution.py:99
  7.9 498.2 %all-reduce.3.cloned.1.call-start = ((), (), s32[]{:S(2)}) async-start(), calls=%async_computation.1 | async-start | bytes 8388608 | tf_op jit(solution)/shard_map/psum | solution.py:19
  8.0 16.9 %collective-permute-start = (f32[16,32,512]{2,1,0:T(8,128)}, f32[16,32,512]{2,1,0:T(8,128)S(1)}, u32[]{:S(2)}, u32[]{:S(2)}) collective-permute-start(f32[16,32,512]{2,1,0:T(8,128)} %param.7), channel_id=1, source_target_pairs={{0,1},{1,2},{2,3},{3,4},{4,5},{5,6},{6,7},{7,8},{8,9},{9,10},{10,1... | collective-permute-start | bytes 3145736 | tf_op jit(solution)/shard_map/ppermute | solution.py:11
  24.8 20.2 %collective-permute-start.1 = (f32[16,32,512]{2,1,0:T(8,128)S(1)}, f32[16,32,512]{2,1,0:T(8,128)S(1)}, u32[]{:S(2)}, u32[]{:S(2)}) collective-permute-start(f32[16,32,512]{2,1,0:T(8,128)S(1)} %collective-permute-done), channel_id=1, source_target_pairs={{0,1},{1,2},{2,3},{3,4},{4,5},{5,6},{6,7},{7,8},{8,9},{9,10},{10,1... | collective-permute-start | bytes 3145736 | tf_op jit(solution)/shard_map/ppermute | solution.py:11
  45.0 22.9 %collective-permute-start.2 = (f32[16,32,512]{2,1,0:T(8,128)S(1)}, f32[16,32,512]{2,1,0:T(8,128)S(1)}, u32[]{:S(2)}, u32[]{:S(2)}) collective-permute-start(f32[16,32,512]{2,1,0:T(8,128)S(1)} %collective-permute-done.1), channel_id=1, source_target_pairs={{0,1},{1,2},{2,3},{3,4},{4,5},{5,6},{6,7},{7,8},{8,9},{9,10},{10,1... | collective-permute-start | bytes 3145736 | tf_op jit(solution)/shard_map/ppermute | solution.py:11
  67.9 1.0 copy-start.6
  69.0 24.1 %collective-permute-start.3 = (f32[16,32,512]{2,1,0:T(8,128)S(1)}, f32[16,32,512]{2,1,0:T(8,128)S(1)}, u32[]{:S(2)}, u32[]{:S(2)}) collective-permute-start(f32[16,32,512]{2,1,0:T(8,128)S(1)} %collective-permute-done.2), channel_id=1, source_target_pairs={{0,1},{1,2},{2,3},{3,4},{4,5},{5,6},{6,7},{7,8},{8,9},{9,10},{10,1... | collective-permute-start | bytes 3145736 | tf_op jit(solution)/shard_map/ppermute | solution.py:11
  93.1 1.0 copy-start.8
  94.1 39.5 %collective-permute-start.4 = (f32[16,32,512]{2,1,0:T(8,128)S(1)}, f32[16,32,512]{2,1,0:T(8,128)S(1)}, u32[]{:S(2)}, u32[]{:S(2)}) collective-permute-start(f32[16,32,512]{2,1,0:T(8,128)S(1)} %collective-permute-done.3), channel_id=1, source_target_pairs={{0,1},{1,2},{2,3},{3,4},{4,5},{5,6},{6,7},{7,8},{8,9},{9,10},{10,1... | collective-permute-start | bytes 3145736 | tf_op jit(solution)/shard_map/ppermute | solution.py:11
  133.6 1.0 copy-start.10
  134.6 39.5 %collective-permute-start.5 = (f32[16,32,512]{2,1,0:T(8,128)S(1)}, f32[16,32,512]{2,1,0:T(8,128)S(1)}, u32[]{:S(2)}, u32[]{:S(2)}) collective-permute-start(f32[16,32,512]{2,1,0:T(8,128)S(1)} %collective-permute-done.4), channel_id=1, source_target_pairs={{0,1},{1,2},{2,3},{3,4},{4,5},{5,6},{6,7},{7,8},{8,9},{9,10},{10,1... | collective-permute-start | bytes 3145736 | tf_op jit(solution)/shard_map/ppermute | solution.py:11
  174.1 1.0 copy-start.12
  175.1 16.9 %collective-permute-start.6 = (f32[16,32,512]{2,1,0:T(8,128)S(1)}, f32[16,32,512]{2,1,0:T(8,128)S(1)}, u32[]{:S(2)}, u32[]{:S(2)}) collective-permute-start(f32[16,32,512]{2,1,0:T(8,128)S(1)} %collective-permute-done.5), channel_id=1, source_target_pairs={{0,1},{1,2},{2,3},{3,4},{4,5},{5,6},{6,7},{7,8},{8,9},{9,10},{10,1... | collective-permute-start | bytes 3145736 | tf_op jit(solution)/shard_map/ppermute | solution.py:11
  192.0 1.0 copy-start.14
  193.0 16.9 %collective-permute-start.7 = (f32[16,32,512]{2,1,0:T(8,128)S(1)}, f32[16,32,512]{2,1,0:T(8,128)S(1)}, u32[]{:S(2)}, u32[]{:S(2)}) collective-permute-start(f32[16,32,512]{2,1,0:T(8,128)S(1)} %collective-permute-done.6), channel_id=1, source_target_pairs={{0,1},{1,2},{2,3},{3,4},{4,5},{5,6},{6,7},{7,8},{8,9},{9,10},{10,1... | collective-permute-start | bytes 3145736 | tf_op jit(solution)/shard_map/ppermute | solution.py:11
  209.9 1.0 copy-start.16
  210.9 16.9 %collective-permute-start.8 = (f32[16,32,512]{2,1,0:T(8,128)S(1)}, f32[16,32,512]{2,1,0:T(8,128)S(1)}, u32[]{:S(2)}, u32[]{:S(2)}) collective-permute-start(f32[16,32,512]{2,1,0:T(8,128)S(1)} %collective-permute-done.7), channel_id=1, source_target_pairs={{0,1},{1,2},{2,3},{3,4},{4,5},{5,6},{6,7},{7,8},{8,9},{9,10},{10,1... | collective-permute-start | bytes 3145736 | tf_op jit(solution)/shard_map/ppermute | solution.py:11
  227.8 1.0 copy-start.18
  228.8 16.9 %collective-permute-start.9 = (f32[16,32,512]{2,1,0:T(8,128)S(1)}, f32[16,32,512]{2,1,0:T(8,128)S(1)}, u32[]{:S(2)}, u32[]{:S(2)}) collective-permute-start(f32[16,32,512]{2,1,0:T(8,128)S(1)} %collective-permute-done.8), channel_id=1, source_target_pairs={{0,1},{1,2},{2,3},{3,4},{4,5},{5,6},{6,7},{7,8},{8,9},{9,10},{10,1... | collective-permute-start | bytes 3145736 | tf_op jit(solution)/shard_map/ppermute | solution.py:11
  245.7 1.0 copy-start.20
  246.8 16.9 %collective-permute-start.10 = (f32[16,32,512]{2,1,0:T(8,128)S(1)}, f32[16,32,512]{2,1,0:T(8,128)S(1)}, u32[]{:S(2)}, u32[]{:S(2)}) collective-permute-start(f32[16,32,512]{2,1,0:T(8,128)S(1)} %collective-permute-done.9), channel_id=1, source_target_pairs={{0,1},{1,2},{2,3},{3,4},{4,5},{5,6},{6,7},{7,8},{8,9},{9,10},{10,1... | collective-permute-start | bytes 3145736 | tf_op jit(solution)/shard_map/ppermute | solution.py:11
  263.7 1.0 copy-start.22
  264.6 16.9 %collective-permute-start.11 = (f32[16,32,512]{2,1,0:T(8,128)S(1)}, f32[16,32,512]{2,1,0:T(8,128)S(1)}, u32[]{:S(2)}, u32[]{:S(2)}) collective-permute-start(f32[16,32,512]{2,1,0:T(8,128)S(1)} %collective-permute-done.10), channel_id=1, source_target_pairs={{0,1},{1,2},{2,3},{3,4},{4,5},{5,6},{6,7},{7,8},{8,9},{9,10},{10,1... | collective-permute-start | bytes 3145736 | tf_op jit(solution)/shard_map/ppermute | solution.py:11
  281.6 1.0 copy-start.24
  282.5 16.9 %collective-permute-start.12 = (f32[16,32,512]{2,1,0:T(8,128)S(1)}, f32[16,32,512]{2,1,0:T(8,128)S(1)}, u32[]{:S(2)}, u32[]{:S(2)}) collective-permute-start(f32[16,32,512]{2,1,0:T(8,128)S(1)} %collective-permute-done.11), channel_id=1, source_target_pairs={{0,1},{1,2},{2,3},{3,4},{4,5},{5,6},{6,7},{7,8},{8,9},{9,10},{10,1... | collective-permute-start | bytes 3145736 | tf_op jit(solution)/shard_map/ppermute | solution.py:11
  299.5 1.0 copy-start.26
  300.4 17.1 %collective-permute-start.13 = (f32[16,32,512]{2,1,0:T(8,128)S(1)}, f32[16,32,512]{2,1,0:T(8,128)}, u32[]{:S(2)}, u32[]{:S(2)}) collective-permute-start(f32[16,32,512]{2,1,0:T(8,128)S(1)} %collective-permute-done.12), channel_id=1, source_target_pairs={{0,1},{1,2},{2,3},{3,4},{4,5},{5,6},{6,7},{7,8},{8,9},{9,10},{10,1... | collective-permute-start | bytes 3145736 | tf_op jit(solution)/shard_map/ppermute | solution.py:11
  317.5 17.2 %collective-permute-start.14 = (f32[16,32,512]{2,1,0:T(8,128)}, f32[16,32,512]{2,1,0:T(8,128)}, u32[]{:S(2)}, u32[]{:S(2)}) collective-permute-start(f32[16,32,512]{2,1,0:T(8,128)} %collective-permute-done.13), channel_id=1, source_target_pairs={{0,1},{1,2},{2,3},{3,4},{4,5},{5,6},{6,7},{7,8},{8,9},{9,10},{10,1... | collective-permute-start | bytes 3145736 | tf_op jit(solution)/shard_map/ppermute | solution.py:11
  317.5 38.7 %copy-start.27 = (f32[16,32,512]{2,1,0:T(8,128)S(1)}, f32[16,32,512]{2,1,0:T(8,128)}, u32[]{:S(2)}) copy-start(f32[16,32,512]{2,1,0:T(8,128)} %copy-done.26) | copy-start | bytes 3145732
  317.5 38.8 %copy-start.25 = (f32[16,32,512]{2,1,0:T(8,128)S(1)}, f32[16,32,512]{2,1,0:T(8,128)}, u32[]{:S(2)}) copy-start(f32[16,32,512]{2,1,0:T(8,128)} %copy-done.24) | copy-start | bytes 3145732
  317.5 38.9 %copy-start.23 = (f32[16,32,512]{2,1,0:T(8,128)S(1)}, f32[16,32,512]{2,1,0:T(8,128)}, u32[]{:S(2)}) copy-start(f32[16,32,512]{2,1,0:T(8,128)} %copy-done.22) | copy-start | bytes 3145732
  317.5 39.0 %copy-start.21 = (f32[16,32,512]{2,1,0:T(8,128)S(1)}, f32[16,32,512]{2,1,0:T(8,128)}, u32[]{:S(2)}) copy-start(f32[16,32,512]{2,1,0:T(8,128)} %copy-done.20) | copy-start | bytes 3145732
  317.5 39.1 %copy-start.19 = (f32[16,32,512]{2,1,0:T(8,128)S(1)}, f32[16,32,512]{2,1,0:T(8,128)}, u32[]{:S(2)}) copy-start(f32[16,32,512]{2,1,0:T(8,128)} %copy-done.18) | copy-start | bytes 3145732
  317.5 39.2 %copy-start.17 = (f32[16,32,512]{2,1,0:T(8,128)S(1)}, f32[16,32,512]{2,1,0:T(8,128)}, u32[]{:S(2)}) copy-start(f32[16,32,512]{2,1,0:T(8,128)} %copy-done.16) | copy-start | bytes 3145732
  317.5 39.3 %copy-start.15 = (f32[16,32,512]{2,1,0:T(8,128)S(1)}, f32[16,32,512]{2,1,0:T(8,128)}, u32[]{:S(2)}) copy-start(f32[16,32,512]{2,1,0:T(8,128)} %copy-done.14) | copy-start | bytes 3145732
  317.5 39.4 %copy-start.13 = (f32[16,32,512]{2,1,0:T(8,128)S(1)}, f32[16,32,512]{2,1,0:T(8,128)}, u32[]{:S(2)}) copy-start(f32[16,32,512]{2,1,0:T(8,128)} %copy-done.12) | copy-start | bytes 3145732
  317.5 39.5 %copy-start.11 = (f32[16,32,512]{2,1,0:T(8,128)S(1)}, f32[16,32,512]{2,1,0:T(8,128)}, u32[]{:S(2)}) copy-start(f32[16,32,512]{2,1,0:T(8,128)} %copy-done.10) | copy-start | bytes 3145732
  317.6 39.6 %copy-start.9 = (f32[16,32,512]{2,1,0:T(8,128)S(1)}, f32[16,32,512]{2,1,0:T(8,128)}, u32[]{:S(2)}) copy-start(f32[16,32,512]{2,1,0:T(8,128)} %copy-done.8) | copy-start | bytes 3145732
  317.6 39.7 %copy-start.7 = (f32[16,32,512]{2,1,0:T(8,128)S(1)}, f32[16,32,512]{2,1,0:T(8,128)}, u32[]{:S(2)}) copy-start(f32[16,32,512]{2,1,0:T(8,128)} %copy-done.6) | copy-start | bytes 3145732
  357.7 11.1 copy-start.2
  621.3 45.0 %copy-start.3 = (f32[2,512,512]{2,1,0:T(8,128)S(1)}, f32[2,512,512]{2,1,0:T(8,128)}, u32[]{:S(2)}) copy-start(f32[2,512,512]{2,1,0:T(8,128)} %get-tuple-element.7) | copy-start | bytes 6291460
  633.5 193.3 %collective-permute-start.15 = (f32[8448,256]{0,1:T(8,128)}, f32[8448,256]{0,1:T(8,128)}, u32[]{:S(2)}, u32[]{:S(2)}) collective-permute-start(f32[8448,256]{0,1:T(8,128)} %get-tuple-element.11), channel_id=1, source_target_pairs={{0,1},{1,2},{2,3},{3,4},{4,5},{5,6},{6,7},{7,8},{8,9},{9,10},{10,1... | collective-permute-start | bytes 25952264 | tf_op jit(solution)/shard_map/ppermute | solution.py:34
  633.5 213.7 %collective-permute-start.16 = (f32[8448,256]{0,1:T(8,128)}, f32[8448,256]{0,1:T(8,128)}, u32[]{:S(2)}, u32[]{:S(2)}) collective-permute-start(f32[8448,256]{0,1:T(8,128)} %get-tuple-element.12), channel_id=1, source_target_pairs={{1,0},{2,1},{3,2},{4,3},{5,4},{6,5},{7,6},{8,7},{9,8},{10,9},{11,1... | collective-permute-start | bytes 25952264 | tf_op jit(solution)/shard_map/ppermute | solution.py:37
  650.7 548.5 %collective-permute-start.19 = (f32[1,512,512]{2,1,0:T(8,128)}, f32[1,512,512]{2,1,0:T(8,128)}, u32[]{:S(2)}, u32[]{:S(2)}) collective-permute-start(f32[1,512,512]{2,1,0:T(8,128)} %constant_dynamic-slice_fusion), channel_id=1, source_target_pairs={{16,0},{0,16},{17,1},{1,17},{18,2},{2,18},{19,3},{3,19},{20,4},{4,... | collective-permute-start | bytes 3145736 | tf_op jit(solution)/shard_map/ppermute | solution.py:25
  666.5 180.7 %collective-permute-start.17 = (f32[1,512,512]{2,1,0:T(8,128)S(1)}, f32[1,512,512]{2,1,0:T(8,128)S(1)}, u32[]{:S(2)}, u32[]{:S(2)}) collective-permute-start(f32[1,512,512]{2,1,0:T(8,128)S(1)} %get-tuple-element.14), channel_id=1, source_target_pairs={{1,0},{2,1},{3,2},{4,3},{5,4},{6,5},{7,6},{8,7},{9,8},{10,9},{11,1... | collective-permute-start | bytes 3145736 | tf_op jit(solution)/shard_map/ppermute | solution.py:25
  705.9 161.7 %copy-start.1 = (f32[8448,512]{0,1:T(8,128)}, f32[8448,512]{0,1:T(8,128)S(1)}, u32[]{:S(2)}) copy-start(f32[8448,512]{0,1:T(8,128)S(1)} %fusion.12) | copy-start | bytes 51904516
  893.9 305.4 %collective-permute-start.20 = (f32[256,1024]{0,1:T(8,128)}, f32[256,1024]{0,1:T(8,128)}, u32[]{:S(2)}, u32[]{:S(2)}) collective-permute-start(f32[256,1024]{0,1:T(8,128)} %get-tuple-element.9), channel_id=1, source_target_pairs={{16,0},{0,16},{17,1},{1,17},{18,2},{2,18},{19,3},{3,19},{20,4},{4,... | collective-permute-start | bytes 3145736 | tf_op jit(solution)/shard_map/ppermute | solution.py:37
  895.1 298.9 %collective-permute-start.18 = (f32[256,1024]{0,1:T(8,128)}, f32[256,1024]{0,1:T(8,128)}, u32[]{:S(2)}, u32[]{:S(2)}) collective-permute-start(f32[256,1024]{0,1:T(8,128)} %get-tuple-element.10), channel_id=1, source_target_pairs={{0,16},{16,0},{1,17},{17,1},{2,18},{18,2},{3,19},{19,3},{4,20},{20... | collective-permute-start | bytes 3145736 | tf_op jit(solution)/shard_map/ppermute | solution.py:34
  1169.3 23.4 %copy-start.4 = (f32[256,1024]{0,1:T(8,128)S(1)}, f32[256,1024]{0,1:T(8,128)}, u32[]{:S(2)}) copy-start(f32[256,1024]{0,1:T(8,128)} %get-tuple-element.8) | copy-start | bytes 3145732
  1169.3 24.7 %copy-start.28 = (f32[512,512]{1,0:T(8,128)S(1)}, f32[512,512]{1,0:T(8,128)}, u32[]{:S(2)}) copy-start(f32[512,512]{1,0:T(8,128)} %fusion.35) | copy-start | bytes 3145732
  1194.0 11.2 copy-start
Sparse Core Ops, SparseCore 0:
  10.2 154.8 all-gather.1
  373.6 119.1 all-reduce.2
